TPU v7x, 128 devices: a whole 4x4x4 slice. The times are simulated.
128 devices in a mesh: tok: 16 (over y, z), head: 8 (over x, core).
Axes of the slice: x: 4, y: 4, z: 4, core: 2. Of those that a mesh axis runs over, the one named last changes fastest.
Arguments:
- prefill_states: bfloat16 [4, 2048, 2048], P(None, 'tok'), may hold values from -6 to 6
- decode_states: bfloat16 [128, 2048], P('tok'), may hold values from -6 to 6
- attn_gain: float32 [2048], replicated, may hold values from 0.1 to 1.9
- w_qkv: bfloat16 [2048, 3, 2048], P(None, None, 'head'), may hold values from -0.125 to 0.125
- w_out: bfloat16 [2048, 2048], P('head'), may hold values from -0.125 to 0.125
- ffn_gain: float32 [2048], replicated, may hold values from 0.1 to 1.9
- w_gate_up: bfloat16 [2048, 2, 5120], P(None, None, 'tok'), may hold values from -0.125 to 0.125
- w_down: bfloat16 [5120, 2048], P('tok'), may hold values from -0.078125 to 0.078125
- prefill_pool: bfloat16 [768, 128, 1024], P('tok', None, 'head')
- prefill_pages: int32 [16, 48], P('tok'), may hold values from 0 to 47, as said below
- prefill_lengths: int32 [4], replicated, may hold values from 1 to 6144, as said below
- prefill_home: int32 [16], replicated, may hold values from 0 to 15, each once
- decode_pool: bfloat16 [1024, 128, 4096], P('tok', None, 'head')
- decode_pages: int32 [128, 32], P('tok'), may hold values from 0 to 63, as said below
- decode_lengths: int32 [128], P('tok'), may hold values from 1 to 4096, as said below
- decode_home: int32 [128], replicated, may hold values from 0 to 127, each once
Outputs:
- prefill_out: bfloat16 [4, 2048, 2048], P(None, ('tok', 'head'))
- decode_out: bfloat16 [128, 2048], P(('tok', 'head'))
Inputs may be any that keep to these rules, and one draw needn't show every extreme that they name: `prefill_pages`: each row is an ordering of all 48 pages of the prefill pool on that row's tok index. `prefill_lengths`: one prefill request has exactly 6144 cached tokens. `decode_pages`: slot s lies on tok index s // 8; within one tok index the first ceil(length / 128) pages of its slots are all different. `decode_lengths`: every tok index hosts one decode request of exactly 4096 cached tokens.
All inputs are finite; a program needn't handle non-finite values.
Results may differ from a plain program's by a relative error of at most 0.017.
The roundings to bfloat16 on the way count: a program that leaves them out, or rounds other values in their place, can miss the bound.
Values may be sent and summed in bfloat16 or wider, within the bound.
A program may use at most 128 MiB of HBM per device.

v0:
```python
import math
import jax
import jax.numpy as jnp
from jax import lax
from jax.sharding import PartitionSpec as P

HD = 64
EPSILON = 1e-06
SCALE = 0.125
MASKED = -1e30


def rms_norm(rows, gain):
    values = rows.astype(jnp.float32)
    inverse = lax.rsqrt(jnp.mean(values * values, axis=-1, keepdims=True) + EPSILON)
    return (values * inverse * gain).astype(jnp.bfloat16)


def inner(left, right):
    return lax.dot_general(
        left, right, (((1,), (1,)), ((), ())), preferred_element_type=jnp.float32
    )


def shards(
    prefill_states,
    decode_states,
    attn_gain,
    w_qkv,
    w_out,
    ffn_gain,
    w_gate_up,
    w_down,
    prefill_pool,
    prefill_pages,
    prefill_lengths,
    prefill_home,
    decode_pool,
    decode_pages,
    decode_lengths,
    decode_home,
):
    n_tok = lax.axis_size("tok")
    n_head = lax.axis_size("head")
    my_tok = lax.axis_index("tok")
    my_head = lax.axis_index("head")
    requests, positions, width = prefill_states.shape
    hosted = decode_states.shape[0]
    heads_per = w_qkv.shape[2] // HD
    stretch = positions * n_tok
    units = requests * heads_per
    features = heads_per * HD
    normed_pre = rms_norm(prefill_states, attn_gain).reshape(requests * positions, width)
    normed_dec = rms_norm(decode_states, attn_gain)
    normed = jnp.concatenate([normed_pre, normed_dec], axis=0)
    projected = jnp.dot(
        normed, w_qkv.reshape(width, 3 * features), preferred_element_type=jnp.float32
    ).astype(jnp.bfloat16)
    proj_pre = projected[: requests * positions].reshape(requests, positions, 3, heads_per, HD)
    proj_dec = projected[requests * positions :]
    unit_ids = jnp.arange(units, dtype=jnp.int32)
    host_ids = jnp.arange(n_tok, dtype=jnp.int32)
    hosted_unit = jnp.sum(
        jnp.where(prefill_home[None, :] == host_ids[:, None], unit_ids[None, :], 0), axis=1
    )
    by_unit = jnp.transpose(proj_pre, (0, 3, 1, 2, 4)).reshape(units, positions * 3 * HD)
    outgoing = jnp.take(by_unit, hosted_unit, axis=0)
    pre_cols = positions * 3 * HD
    spread = jnp.broadcast_to(
        proj_dec.reshape(1, hosted * 3 * features), (n_tok, hosted * 3 * features)
    )
    outgoing = jnp.concatenate([outgoing, spread], axis=1)
    arrived = lax.all_to_all(outgoing, "tok", split_axis=0, concat_axis=0, tiled=True)
    arrived_dec = arrived[:, pre_cols:].reshape(n_tok * hosted, 3, heads_per, HD)
    arrived_pre = arrived[:, :pre_cols].reshape(stretch, 3, HD)
    query_rows = arrived_pre[:, 0]
    key_rows = arrived_pre[:, 1]
    value_rows = arrived_pre[:, 2]
    my_unit = hosted_unit[my_tok]
    length = prefill_lengths[my_unit // heads_per]
    cache = jnp.take(prefill_pool, prefill_pages[0], axis=0).reshape(-1, 2 * HD)
    cache_keys = cache[:, :HD]
    cache_values = cache[:, HD:]
    span = cache.shape[0]
    block = math.gcd(stretch, 512)

    def attend(start):
        rows = lax.dynamic_slice_in_dim(query_rows, start, block, 0)
        score_cache = inner(rows, cache_keys) * SCALE
        score_cache = jnp.where(jnp.arange(span)[None, :] < length, score_cache, MASKED)
        score_stretch = inner(rows, key_rows) * SCALE
        row_pos = start + jnp.arange(block)[:, None]
        score_stretch = jnp.where(jnp.arange(stretch)[None, :] <= row_pos, score_stretch, MASKED)
        top = jnp.maximum(
            jnp.max(score_cache, axis=1, keepdims=True),
            jnp.max(score_stretch, axis=1, keepdims=True),
        )
        weight_cache = jnp.exp(score_cache - top)
        weight_stretch = jnp.exp(score_stretch - top)
        total = jnp.sum(weight_cache, axis=1, keepdims=True) + jnp.sum(
            weight_stretch, axis=1, keepdims=True
        )
        mixed = jnp.dot(
            weight_cache.astype(jnp.bfloat16), cache_values, preferred_element_type=jnp.float32
        )
        mixed = mixed + jnp.dot(
            weight_stretch.astype(jnp.bfloat16), value_rows, preferred_element_type=jnp.float32
        )
        return (mixed / total).astype(jnp.bfloat16)

    starts = jnp.arange(stretch // block, dtype=jnp.int32) * block
    attn_unit = lax.map(attend, starts).reshape(stretch, HD)
    slots = my_tok * hosted + jnp.arange(hosted, dtype=jnp.int32)
    all_requests = jnp.arange(decode_home.shape[0], dtype=jnp.int32)
    anchor = jnp.sum(
        jnp.where(decode_home[None, :] == slots[:, None], all_requests[None, :], 0), axis=1
    )
    mine = jnp.take(arrived_dec, anchor, axis=0)

    def decode_one(operands):
        pages, slot_length, rows = operands
        cache_slot = jnp.take(decode_pool, pages, axis=0).reshape(-1, heads_per, 2 * HD)
        query = rows[0]
        scores = (
            jnp.einsum(
                "hd,khd->hk", query, cache_slot[:, :, :HD], preferred_element_type=jnp.float32
            )
            * SCALE
        )
        scores = jnp.where(jnp.arange(cache_slot.shape[0])[None, :] < slot_length, scores, MASKED)
        own_score = (
            jnp.sum(query.astype(jnp.float32) * rows[1].astype(jnp.float32), axis=1, keepdims=True)
            * SCALE
        )
        top = jnp.maximum(jnp.max(scores, axis=1, keepdims=True), own_score)
        weights = jnp.exp(scores - top)
        own_weight = jnp.exp(own_score - top)
        total = jnp.sum(weights, axis=1, keepdims=True) + own_weight
        mixed = jnp.einsum(
            "hk,khd->hd",
            weights.astype(jnp.bfloat16),
            cache_slot[:, :, HD:],
            preferred_element_type=jnp.float32,
        )
        mixed = mixed + own_weight.astype(jnp.bfloat16).astype(jnp.float32) * rows[2].astype(
            jnp.float32
        )
        return (mixed / total).astype(jnp.bfloat16).reshape(features)

    decode_attn = lax.map(decode_one, (decode_pages, decode_lengths, mine))
    backward = attn_unit.reshape(n_tok, positions * HD)
    back_cols = positions * HD
    spread_back = jnp.broadcast_to(
        decode_attn.reshape(1, hosted * features), (n_tok, hosted * features)
    )
    backward = jnp.concatenate([backward, spread_back], axis=1)
    returned = lax.all_to_all(backward, "tok", split_axis=0, concat_axis=0, tiled=True)
    by_slot = returned[:, back_cols:].reshape(n_tok * hosted, features)
    my_slots = lax.dynamic_slice_in_dim(decode_home, my_tok * hosted, hosted, 0)
    attn_dec = jnp.take(by_slot, my_slots, axis=0)
    attn_pre = jnp.take(returned[:, :back_cols], prefill_home, axis=0).reshape(
        requests, heads_per, positions, HD
    )
    block_rows = positions // n_head
    decode_share = hosted // n_head
    per = requests * block_rows + decode_share
    pre_rows = jnp.transpose(attn_pre, (0, 2, 1, 3)).reshape(requests, n_head, block_rows, features)
    pre_rows = jnp.transpose(pre_rows, (1, 0, 2, 3)).reshape(
        n_head, requests * block_rows, features
    )
    dec_rows = attn_dec.reshape(n_head, decode_share, features)
    ordered = jnp.concatenate([pre_rows, dec_rows], axis=1).reshape(n_head * per, features)
    mixed_rows = lax.psum_scatter(
        jnp.dot(ordered, w_out, preferred_element_type=jnp.float32).astype(jnp.bfloat16),
        "head",
        scatter_dimension=0,
        tiled=True,
    ).astype(jnp.float32)
    own_pre = lax.dynamic_slice_in_dim(prefill_states, my_head * block_rows, block_rows, 1).reshape(
        requests * block_rows, width
    )
    own_dec = lax.dynamic_slice_in_dim(decode_states, my_head * decode_share, decode_share, 0)
    resid = jnp.concatenate([own_pre, own_dec], axis=0).astype(jnp.float32) + mixed_rows
    normed_mid = rms_norm(resid, ffn_gain)
    piece = lax.all_gather(normed_mid, "tok", axis=0, tiled=True)
    gate = jnp.dot(piece, w_gate_up[:, 0], preferred_element_type=jnp.float32)
    upper = jnp.dot(piece, w_gate_up[:, 1], preferred_element_type=jnp.float32)
    hidden = (jax.nn.gelu(gate, approximate=True) * upper).astype(jnp.bfloat16)
    summed = lax.psum(
        jnp.dot(hidden, w_down, preferred_element_type=jnp.float32).astype(jnp.bfloat16), "tok"
    ).astype(jnp.float32)
    ffn_rows = lax.dynamic_slice_in_dim(summed, my_tok * per, per, 0)
    result = (resid + ffn_rows).astype(jnp.bfloat16)
    prefill_out = result[: requests * block_rows].reshape(requests, block_rows, width)
    decode_out = result[requests * block_rows :]
    return (prefill_out, decode_out)


def solution(mesh):
    placed = (
        P(None, "tok", None),
        P("tok", None),
        P(),
        P(None, None, "head"),
        P("head", None),
        P(),
        P(None, None, "tok"),
        P("tok", None),
        P("tok", None, "head"),
        P("tok", None),
        P(),
        P(),
        P("tok", None, "head"),
        P("tok", None),
        P("tok"),
        P(),
    )
    return jax.shard_map(
        shards,
        mesh=mesh,
        in_specs=placed,
        out_specs=(P(None, ("tok", "head"), None), P(("tok", "head"), None)),
        check_vma=False,
    )
```

profile of v0, /device:TPU:1, one launch (start us, length us, event | category | flops | bytes accessed | tf_op | source)
XLA Modules:
  0.0 700.8 jit_solution(3987301994790291985)
XLA Ops:
  16.1 4.7 copy.74
  20.8 4.4 fusion.67
  36.3 9.1 %all-to-all-start = ((bf16[16,2,15360]{2,1,0:T(2,128)(2,1)}), bf16[16,2,15360]{2,1,0:T(2,128)(2,1)}, u32[]{:S(2)}, u32[]{:S(2)}) async-start(bf16[16,2,15360]{2,1,0:T(2,128)(2,1)} %reshape.373), calls=%async_computation | async-start | bytes 1966080 | tf_op jit(solution)/shard_map/all_to_all | solution.py:73
  61.6 4.2 reshape.374
  67.5 310.7 %while.21 = (s32[]{:T(128)}, bf16[8,256]{1,0:T(8,128)(2,1)S(1)}, s32[8]{0:T(128)S(1)}, bf16[8,3,4,64]{3,2,1,0:T(4,128)(2,1)S(1)}, s32[8,32]{1,0:T(8,128)}, /*ind...) while((s32[]{:T(128)}, bf16[8,256]{1,0:T(8,128)(2,1)S(1)}, s32[8]{0:T(128)S(1)}, ...), condition=%wide.region_14.15_spmd, body=%wide.region_10.14_spmd.sunk | while | flops 6430264 | bytes 38044244 | solution.py:150
  70.4 6.1 gather_fusion
  76.6 6.9 gather.55
  83.5 16.5 %broadcast_select_fusion.4 = bf16[4096,4,128]{2,1,0:T(4,128)(2,1)S(1)} fusion(bf16[4096,4,128]{2,1,0:T(4,128)(2,1)} %gather.55, pred[4096]{0:T(1024)(128)(4,1)S(1)} %broadcast_bitcast_fusion.3), kind=kLoop, calls=%fused_computation.38.clone.1 | loop fusion | flops 2097152 | bytes 8392704 | tf_op jit(solution)/shard_map/while/body/eval_jaxpr/jit(_take)/select_n | solution.py:122
  100.0 3.8 fusion.145
  109.3 6.1 gather_fusion
  115.4 6.9 gather.55
  122.3 16.5 %broadcast_select_fusion.4 = bf16[4096,4,128]{2,1,0:T(4,128)(2,1)S(1)} fusion(bf16[4096,4,128]{2,1,0:T(4,128)(2,1)} %gather.55, pred[4096]{0:T(1024)(128)(4,1)S(1)} %broadcast_bitcast_fusion.3), kind=kLoop, calls=%fused_computation.38.clone.1 | loop fusion | flops 2097152 | bytes 8392704 | tf_op jit(solution)/shard_map/while/body/eval_jaxpr/jit(_take)/select_n | solution.py:122
  138.8 3.8 fusion.145
  148.1 6.1 gather_fusion
  154.2 6.9 gather.55
  161.2 16.5 %broadcast_select_fusion.4 = bf16[4096,4,128]{2,1,0:T(4,128)(2,1)S(1)} fusion(bf16[4096,4,128]{2,1,0:T(4,128)(2,1)} %gather.55, pred[4096]{0:T(1024)(128)(4,1)S(1)} %broadcast_bitcast_fusion.3), kind=kLoop, calls=%fused_computation.38.clone.1 | loop fusion | flops 2097152 | bytes 8392704 | tf_op jit(solution)/shard_map/while/body/eval_jaxpr/jit(_take)/select_n | solution.py:122
  177.6 3.8 fusion.145
  187.0 6.1 gather_fusion
  193.1 6.9 gather.55
  200.0 16.5 %broadcast_select_fusion.4 = bf16[4096,4,128]{2,1,0:T(4,128)(2,1)S(1)} fusion(bf16[4096,4,128]{2,1,0:T(4,128)(2,1)} %gather.55, pred[4096]{0:T(1024)(128)(4,1)S(1)} %broadcast_bitcast_fusion.3), kind=kLoop, calls=%fused_computation.38.clone.1 | loop fusion | flops 2097152 | bytes 8392704 | tf_op jit(solution)/shard_map/while/body/eval_jaxpr/jit(_take)/select_n | solution.py:122
  216.5 3.8 fusion.145
  225.8 6.1 gather_fusion
  231.9 6.9 gather.55
  238.8 16.5 %broadcast_select_fusion.4 = bf16[4096,4,128]{2,1,0:T(4,128)(2,1)S(1)} fusion(bf16[4096,4,128]{2,1,0:T(4,128)(2,1)} %gather.55, pred[4096]{0:T(1024)(128)(4,1)S(1)} %broadcast_bitcast_fusion.3), kind=kLoop, calls=%fused_computation.38.clone.1 | loop fusion | flops 2097152 | bytes 8392704 | tf_op jit(solution)/shard_map/while/body/eval_jaxpr/jit(_take)/select_n | solution.py:122
  255.3 3.8 fusion.145
  264.6 6.1 gather_fusion
  270.7 6.9 gather.55
  277.7 16.5 %broadcast_select_fusion.4 = bf16[4096,4,128]{2,1,0:T(4,128)(2,1)S(1)} fusion(bf16[4096,4,128]{2,1,0:T(4,128)(2,1)} %gather.55, pred[4096]{0:T(1024)(128)(4,1)S(1)} %broadcast_bitcast_fusion.3), kind=kLoop, calls=%fused_computation.38.clone.1 | loop fusion | flops 2097152 | bytes 8392704 | tf_op jit(solution)/shard_map/while/body/eval_jaxpr/jit(_take)/select_n | solution.py:122
  303.5 6.1 gather_fusion
  309.6 6.9 gather.55
  316.5 16.5 %broadcast_select_fusion.4 = bf16[4096,4,128]{2,1,0:T(4,128)(2,1)S(1)} fusion(bf16[4096,4,128]{2,1,0:T(4,128)(2,1)} %gather.55, pred[4096]{0:T(1024)(128)(4,1)S(1)} %broadcast_bitcast_fusion.3), kind=kLoop, calls=%fused_computation.38.clone.1 | loop fusion | flops 2097152 | bytes 8392704 | tf_op jit(solution)/shard_map/while/body/eval_jaxpr/jit(_take)/select_n | solution.py:122
  333.0 3.8 fusion.145
  342.3 6.1 gather_fusion
  348.4 6.9 gather.55
  355.3 16.5 %broadcast_select_fusion.4 = bf16[4096,4,128]{2,1,0:T(4,128)(2,1)S(1)} fusion(bf16[4096,4,128]{2,1,0:T(4,128)(2,1)} %gather.55, pred[4096]{0:T(1024)(128)(4,1)S(1)} %broadcast_bitcast_fusion.3), kind=kLoop, calls=%fused_computation.38.clone.1 | loop fusion | flops 2097152 | bytes 8392704 | tf_op jit(solution)/shard_map/while/body/eval_jaxpr/jit(_take)/select_n | solution.py:122
  384.0 76.3 %while.20 = (s32[]{:T(128)}, bf16[4,512,64]{1,2,0:T(8,128)(2,1)}, s32[]{:T(128)}, s32[4]{0:T(128)}, bf16[2048,64]{1,0:T(8,128)(2,1)S(1)}, /*index=5*/bf16[6144,6...) while((s32[]{:T(128)}, bf16[4,512,64]{1,2,0:T(8,128)(2,1)}, ...), condition=%wide.region_8.9_spmd, body=%wide.region_3.8_spmd.sunk | while | flops 1116837376 | bytes 57026836 | solution.py:112
  397.3 4.3 fusion.136
  416.4 4.3 fusion.136
  435.4 4.3 fusion.136
  454.4 4.3 fusion.136
  464.6 6.8 all-to-all-start.1
  473.0 6.1 all-to-all-done.1
  485.0 21.3 %fusion = bf16[72,2048]{1,0:T(8,128)(2,1)S(1)} fusion(bf16[520,2048]{1,0:T(8,128)(2,1)S(1)} %convolution_convert_fusion.1), kind=kCustom, calls=%all-reduce-scatter | all-reduce-scatter fusion | flops 1179649 | bytes 2425344
  514.9 52.3 %all-gather.3.cloned.1.call-done = bf16[16,65,2048]{2,1,0:T(8,128)(2,1)} async-done(((bf16[1,65,2048]{2,1,0:T(8,128)(2,1)}), bf16[16,65,2048]{2,1,0:T(8,128)(2,1)}) %all-gather.3.cloned.1.call-update) | async-done | bytes 4259856 | tf_op jit(solution)/shard_map/all_gather | solution.py:185
  567.1 4.4 reshape.365
  571.6 5.6 fusion.71
  577.2 10.4 %convolution_convert_fusion = bf16[1040,2048]{1,0:T(8,128)(2,1)} fusion(bf16[320,2048]{1,0:T(8,128)(2,1)} %param.27, bf16[1040,2048]{1,0:T(8,128)(2,1)} %reshape.365, f32[1040,320]{0,1:T(8,128)} %fusion.71, bf16[2048,2,320]{0,2,1:T(8,128)(2,1)} %param.26), kind=kOutput, calls=%fused_computation.70 | convolution fusion | flops 2731755520 | bytes 12615680 | tf_op jit(solution)/shard_map/dot_general | solution.py:190
  587.6 103.6 %all-reduce.4.cloned.1.call-done = bf16[1040,2048]{1,0:T(8,128)(2,1)} async-done(((bf16[1040,2048]{1,0:T(8,128)(2,1)}), bf16[1040,2048]{1,0:T(8,128)(2,1)}) %all-reduce.4.cloned.1.call-update) | async-done | bytes 4259856 | tf_op jit(solution)/shard_map/psum | solution.py:189
  (320 shorter events, 165.7 us)
Async XLA Ops:
  7.2 48.0 %copy-start = (bf16[48,128,128]{2,1,0:T(8,128)(2,1)S(1)}, bf16[48,128,128]{2,1,0:T(8,128)(2,1)}, u32[]{:S(2)}) copy-start(bf16[48,128,128]{2,1,0:T(8,128)(2,1)} %param.28) | copy-start | bytes 4718596
  8.1 12.7 %copy-start.11 = (s32[16]{0:T(128)}, s32[16]{0:T(128)S(1)}, u32[]{:S(2)}) copy-start(s32[16]{0:T(128)S(1)} %select_reduce_fusion) | copy-start | bytes 196
  32.4 17.1 %copy-start.9 = (s32[16]{0:T(128)S(1)}, s32[16]{0:T(128)}, u32[]{:S(2)}) copy-start(s32[16]{0:T(128)} %param.31) | copy-start | bytes 196
  32.4 18.2 %copy-start.10 = (s32[128]{0:T(128)S(1)}, s32[128]{0:T(128)}, u32[]{:S(2)}) copy-start(s32[128]{0:T(128)} %param.35) | copy-start | bytes 1540
  32.5 20.4 %copy-start.8 = (u32[128]{0:T(128)S(1)}, u32[128]{0:T(128)}, u32[]{:S(2)}) copy-start(u32[128]{0:T(128)} %constant.188) | copy-start | bytes 1540
  36.3 25.3 %all-to-all-start = ((bf16[16,2,15360]{2,1,0:T(2,128)(2,1)}), bf16[16,2,15360]{2,1,0:T(2,128)(2,1)}, u32[]{:S(2)}, u32[]{:S(2)}) async-start(bf16[16,2,15360]{2,1,0:T(2,128)(2,1)} %reshape.373), calls=%async_computation | async-start | bytes 1966080 | tf_op jit(solution)/shard_map/all_to_all | solution.py:73
  61.6 5.9 copy-start.12
  387.3 3.3 copy-start.2
  397.3 4.3 copy-start.3
  397.3 4.3 copy-start.4
  406.4 3.3 copy-start.2
  416.4 4.3 copy-start.3
  416.4 4.3 copy-start.4
  425.4 3.3 copy-start.2
  435.4 4.3 copy-start.3
  435.4 4.3 copy-start.4
  444.4 3.3 copy-start.2
  454.4 4.3 copy-start.3
  454.4 4.3 copy-start.4
  460.3 20.2 %copy-start.6 = (pred[8]{0:T(512)(128)(4,1)S(1)}, pred[8]{0:T(512)(128)(4,1)}, u32[]{:S(2)}) copy-start(pred[8]{0:T(512)(128)(4,1)} %get-tuple-element.149) | copy-start | bytes 28
  462.8 19.2 %copy-start.7 = (pred[4,4]{1,0:T(4,128)(4,1)S(1)}, pred[4,4]{1,0:T(4,128)(4,1)}, u32[]{:S(2)}) copy-start(pred[4,4]{1,0:T(4,128)(4,1)} %broadcast_in_dim.177) | copy-start | bytes 52
  464.6 14.6 %all-to-all-start.1 = ((bf16[16,2,5120]{2,1,0:T(2,128)(2,1)}), bf16[16,2,5120]{2,1,0:T(2,128)(2,1)S(1)}, u32[]{:S(2)}, u32[]{:S(2)}) async-start(bf16[16,2,5120]{2,1,0:T(2,128)(2,1)} %reshape.375), calls=%async_computation.1 | async-start | bytes 655360 | tf_op jit(solution)/shard_map/all_to_all | solution.py:157
  471.3 95.8 %all-gather.3.cloned.1.call-start = ((), (), s32[]{:S(2)}) async-start(), calls=%async_computation.3 | async-start | bytes 5013504 | tf_op jit(solution)/shard_map/all_gather | solution.py:185
  483.0 30.9 %copy-start.5 = (f32[2048]{0:T(1024)S(1)}, f32[2048]{0:T(1024)}, u32[]{:S(2)}) copy-start(f32[2048]{0:T(1024)} %param.25) | copy-start | bytes 24580
  506.3 6.8 collective-permute-start
  514.8 176.4 %all-reduce.4.cloned.1.call-start = ((), (), s32[]{:S(2)}) async-start(), calls=%async_computation.2 | async-start | bytes 8519680 | tf_op jit(solution)/shard_map/psum | solution.py:189
  577.2 116.5 %copy-start.1 = (bf16[48,128,128]{2,1,0:T(8,128)(2,1)S(1)}, bf16[48,128,128]{2,1,0:T(8,128)(2,1)}, u32[]{:S(2)}) copy-start(bf16[48,128,128]{2,1,0:T(8,128)(2,1)} %param.28) | copy-start | bytes 4718596
Sparse Core Ops, SparseCore 0:
  514.9 52.1 all-gather.2
  587.8 103.4 all-reduce.3
where the time goes:
time: 710 us; the launch traced here: 701 us
  other arithmetic  200 us (28%)
  local copies, waits for them, and re-layouts  193 us (27%)
  waiting for transfers between devices  164 us (23%)
  matrix products  76.3 us (11%)
  blocking collectives  21.3 us (3%)
  starting transfers between devices  19.8 us (3%)
  between operations  17.5 us (2%)
  loops' own time  8.49 us (1%)
    select_n x16, other arithmetic, decode_one(): jnp.take(decode_pool, pages, axis=0).reshape(-1, heads_per, 2 * HD)  137 us
    gather x16, local copies, waits for them, and re-layouts, decode_one(): jnp.take(decode_pool, pages, axis=0).reshape(-1, heads_per, 2 * HD)  104 us
    psum x1, waiting for transfers between devices, shards(): lax.psum(jnp.dot(hidden, w_down, preferred_element_type=jnp.float32).asty...  104 us
    all_gather x1, waiting for transfers between devices, shards(): piece = lax.all_gather(normed_mid, 'tok', axis=0, tiled=True)  52.3 us
    slice x8, local copies, waits for them, and re-layouts, decode_one(): cache_slot[:, :, :HD]  30.5 us
    unnamed x1, blocking collectives  21.3 us
    unnamed x32, local copies, waits for them, and re-layouts  18.4 us
    dot_general x4, matrix products, attend(): jnp.dot(weight_cache.astype(jnp.bfloat16), cache_values, preferred_elemen...  17.3 us
  transfers between devices with their start and end apart: 5, of which 4 were waited for; matrix products, arithmetic and copies ran while one was open for 2% of the time, Pallas kernels for 0%

commit v1 on v0

--- a/solution.py
+++ b/solution.py
@@ -186,8 +186,9 @@
     gate = jnp.dot(piece, w_gate_up[:, 0], preferred_element_type=jnp.float32)
     upper = jnp.dot(piece, w_gate_up[:, 1], preferred_element_type=jnp.float32)
     hidden = (jax.nn.gelu(gate, approximate=True) * upper).astype(jnp.bfloat16)
-    summed = lax.psum(
-        jnp.dot(hidden, w_down, preferred_element_type=jnp.float32).astype(jnp.bfloat16), "tok"
+    define_group_up = lambda q_in: jnp.sum(lax.all_gather(q_in, "tok"), 0)
+    summed = define_group_up(
+        jnp.dot(hidden, w_down, preferred_element_type=jnp.float32).astype(jnp.bfloat16)
     ).astype(jnp.float32)
     ffn_rows = lax.dynamic_slice_in_dim(summed, my_tok * per, per, 0)
     result = (resid + ffn_rows).astype(jnp.bfloat16)

time: 710 us -> 1000 us (1.41)
  waiting for transfers between devices: 164 us -> 434 us
  other arithmetic: 200 us -> 224 us
    all_gather x0 -> x1, waiting for transfers between devices: none -> 374 us  [shards(): define_group_up = lambda q_in: jnp.sum(lax.all_gather(q_in, 'tok'), 0)]
    psum x1 -> x0, waiting for transfers between devices: 104 us -> none  [shards(): lax.psum(jnp.dot(hidden, w_down, preferred_element_type=jnp.float32).asty...]
    reduce_sum x0 -> x1, other arithmetic: none -> 24.6 us  [shards(): define_group_up = lambda q_in: jnp.sum(lax.all_gather(q_in, 'tok'), 0)]
where the time goes in v1:
time: 1000 us; the launch traced here: 995 us
  waiting for transfers between devices  434 us (43%)
  other arithmetic  224 us (22%)
  local copies, waits for them, and re-layouts  193 us (19%)
  matrix products  76 us (8%)
  blocking collectives  21.3 us (2%)
  starting transfers between devices  19.8 us (2%)
  between operations  17.5 us (2%)
    all_gather x1, waiting for transfers between devices, shards(): define_group_up = lambda q_in: jnp.sum(lax.all_gather(q_in, 'tok'), 0)  374 us
    select_n x16, other arithmetic, decode_one(): jnp.take(decode_pool, pages, axis=0).reshape(-1, heads_per, 2 * HD)  137 us
    gather x16, local copies, waits for them, and re-layouts, decode_one(): jnp.take(decode_pool, pages, axis=0).reshape(-1, heads_per, 2 * HD)  104 us
    all_gather x1, waiting for transfers between devices, shards(): piece = lax.all_gather(normed_mid, 'tok', axis=0, tiled=True)  52.3 us
    slice x8, local copies, waits for them, and re-layouts, decode_one(): cache_slot[:, :, :HD]  30.5 us
    reduce_sum x1, other arithmetic, shards(): define_group_up = lambda q_in: jnp.sum(lax.all_gather(q_in, 'tok'), 0)  24.6 us
    unnamed x1, blocking collectives  21.3 us
  transfers between devices with their start and end apart: 5, of which 4 were waited for; matrix products, arithmetic and copies ran while one was open for 2% of the time, Pallas kernels for 0%

profile of v1, /device:TPU:1, one launch (start us, length us, event | category | flops | bytes accessed | tf_op | source)
XLA Modules:
  0.0 995.2 jit_solution(10285119599671011633)
XLA Ops:
  16.1 4.7 copy.74
  20.8 4.4 fusion.67
  36.3 9.1 all-to-all-start
  61.6 4.2 reshape.375
  67.5 310.7 %while.21 = (s32[]{:T(128)}, bf16[8,256]{1,0:T(8,128)(2,1)S(1)}, s32[8]{0:T(128)S(1)}, bf16[8,3,4,64]{3,2,1,0:T(4,128)(2,1)S(1)}, s32[8,32]{1,0:T(8,128)}, /*ind...) while((s32[]{:T(128)}, bf16[8,256]{1,0:T(8,128)(2,1)S(1)}, s32[8]{0:T(128)S(1)}, ...), condition=%wide.region_14.15_spmd, body=%wide.region_10.14_spmd.sunk | while | flops 6430264 | bytes 38044244 | solution.py:150
  70.4 6.1 gather_fusion
  76.6 6.9 gather.55
  83.5 16.5 %broadcast_select_fusion.4 = bf16[4096,4,128]{2,1,0:T(4,128)(2,1)S(1)} fusion(bf16[4096,4,128]{2,1,0:T(4,128)(2,1)} %gather.55, pred[4096]{0:T(1024)(128)(4,1)S(1)} %broadcast_bitcast_fusion.3), kind=kLoop, calls=%fused_computation.38.clone.1 | loop fusion | flops 2097152 | bytes 8392704 | tf_op jit(solution)/shard_map/while/body/eval_jaxpr/jit(_take)/select_n | solution.py:122
  100.0 3.8 fusion.145
  109.3 6.1 gather_fusion
  115.4 6.9 gather.55
  122.3 16.5 %broadcast_select_fusion.4 = bf16[4096,4,128]{2,1,0:T(4,128)(2,1)S(1)} fusion(bf16[4096,4,128]{2,1,0:T(4,128)(2,1)} %gather.55, pred[4096]{0:T(1024)(128)(4,1)S(1)} %broadcast_bitcast_fusion.3), kind=kLoop, calls=%fused_computation.38.clone.1 | loop fusion | flops 2097152 | bytes 8392704 | tf_op jit(solution)/shard_map/while/body/eval_jaxpr/jit(_take)/select_n | solution.py:122
  138.8 3.8 fusion.145
  148.1 6.1 gather_fusion
  154.2 6.9 gather.55
  161.2 16.5 %broadcast_select_fusion.4 = bf16[4096,4,128]{2,1,0:T(4,128)(2,1)S(1)} fusion(bf16[4096,4,128]{2,1,0:T(4,128)(2,1)} %gather.55, pred[4096]{0:T(1024)(128)(4,1)S(1)} %broadcast_bitcast_fusion.3), kind=kLoop, calls=%fused_computation.38.clone.1 | loop fusion | flops 2097152 | bytes 8392704 | tf_op jit(solution)/shard_map/while/body/eval_jaxpr/jit(_take)/select_n | solution.py:122
  177.6 3.8 fusion.145
  187.0 6.1 gather_fusion
  193.1 6.9 gather.55
  200.0 16.5 %broadcast_select_fusion.4 = bf16[4096,4,128]{2,1,0:T(4,128)(2,1)S(1)} fusion(bf16[4096,4,128]{2,1,0:T(4,128)(2,1)} %gather.55, pred[4096]{0:T(1024)(128)(4,1)S(1)} %broadcast_bitcast_fusion.3), kind=kLoop, calls=%fused_computation.38.clone.1 | loop fusion | flops 2097152 | bytes 8392704 | tf_op jit(solution)/shard_map/while/body/eval_jaxpr/jit(_take)/select_n | solution.py:122
  225.8 6.1 gather_fusion
  231.9 6.9 gather.55
  238.8 16.5 %broadcast_select_fusion.4 = bf16[4096,4,128]{2,1,0:T(4,128)(2,1)S(1)} fusion(bf16[4096,4,128]{2,1,0:T(4,128)(2,1)} %gather.55, pred[4096]{0:T(1024)(128)(4,1)S(1)} %broadcast_bitcast_fusion.3), kind=kLoop, calls=%fused_computation.38.clone.1 | loop fusion | flops 2097152 | bytes 8392704 | tf_op jit(solution)/shard_map/while/body/eval_jaxpr/jit(_take)/select_n | solution.py:122
  255.3 3.8 fusion.145
  264.6 6.1 gather_fusion
  270.7 6.9 gather.55
  277.7 16.5 %broadcast_select_fusion.4 = bf16[4096,4,128]{2,1,0:T(4,128)(2,1)S(1)} fusion(bf16[4096,4,128]{2,1,0:T(4,128)(2,1)} %gather.55, pred[4096]{0:T(1024)(128)(4,1)S(1)} %broadcast_bitcast_fusion.3), kind=kLoop, calls=%fused_computation.38.clone.1 | loop fusion | flops 2097152 | bytes 8392704 | tf_op jit(solution)/shard_map/while/body/eval_jaxpr/jit(_take)/select_n | solution.py:122
  303.5 6.1 gather_fusion
  309.6 6.9 gather.55
  316.5 16.5 %broadcast_select_fusion.4 = bf16[4096,4,128]{2,1,0:T(4,128)(2,1)S(1)} fusion(bf16[4096,4,128]{2,1,0:T(4,128)(2,1)} %gather.55, pred[4096]{0:T(1024)(128)(4,1)S(1)} %broadcast_bitcast_fusion.3), kind=kLoop, calls=%fused_computation.38.clone.1 | loop fusion | flops 2097152 | bytes 8392704 | tf_op jit(solution)/shard_map/while/body/eval_jaxpr/jit(_take)/select_n | solution.py:122
  333.0 3.8 fusion.145
  342.3 6.1 gather_fusion
  348.4 6.9 gather.55
  355.3 16.5 %broadcast_select_fusion.4 = bf16[4096,4,128]{2,1,0:T(4,128)(2,1)S(1)} fusion(bf16[4096,4,128]{2,1,0:T(4,128)(2,1)} %gather.55, pred[4096]{0:T(1024)(128)(4,1)S(1)} %broadcast_bitcast_fusion.3), kind=kLoop, calls=%fused_computation.38.clone.1 | loop fusion | flops 2097152 | bytes 8392704 | tf_op jit(solution)/shard_map/while/body/eval_jaxpr/jit(_take)/select_n | solution.py:122
  384.0 76.3 %while.20 = (s32[]{:T(128)}, bf16[4,512,64]{1,2,0:T(8,128)(2,1)}, s32[]{:T(128)}, s32[4]{0:T(128)}, bf16[2048,64]{1,0:T(8,128)(2,1)S(1)}, /*index=5*/bf16[6144,6...) while((s32[]{:T(128)}, bf16[4,512,64]{1,2,0:T(8,128)(2,1)}, ...), condition=%wide.region_8.9_spmd, body=%wide.region_3.8_spmd.sunk | while | flops 1116837376 | bytes 57026836 | solution.py:112
  397.3 4.3 fusion.136
  416.4 4.3 fusion.136
  435.4 4.3 fusion.136
  454.4 4.3 fusion.136
  464.6 6.8 all-to-all-start.1
  473.0 6.1 all-to-all-done.1
  485.0 21.3 %fusion = bf16[72,2048]{1,0:T(8,128)(2,1)S(1)} fusion(bf16[520,2048]{1,0:T(8,128)(2,1)S(1)} %convolution_convert_fusion.1), kind=kCustom, calls=%all-reduce-scatter | all-reduce-scatter fusion | flops 1179649 | bytes 2425344
  514.9 52.3 %all-gather.7.cloned.1.call-done = bf16[16,65,2048]{2,1,0:T(8,128)(2,1)} async-done(((bf16[1,65,2048]{2,1,0:T(8,128)(2,1)}), bf16[16,65,2048]{2,1,0:T(8,128)(2,1)}) %all-gather.7.cloned.1.call-update) | async-done | bytes 4259856 | tf_op jit(solution)/shard_map/all_gather | solution.py:185
  567.1 4.4 reshape.366
  571.6 5.7 fusion.71
  577.3 10.0 %convolution_convert_fusion = bf16[1040,2048]{1,0:T(8,128)(2,1)} fusion(bf16[320,2048]{1,0:T(8,128)(2,1)S(1)} %copy-done.12, bf16[1040,2048]{1,0:T(8,128)(2,1)} %reshape.366, f32[1040,320]{0,1:T(8,128)} %fusion.71, bf16[2048,2,320]{0,2,1:T(8,128)(2,1)} %param.26), kind=kOutput, calls=%fused_computation.70 | convolution fusion | flops 2731755520 | bytes 12615680 | tf_op jit(solution)/shard_map/dot_general | solution.py:191
  587.3 373.8 %all-gather.5.cloned.1.call-done = bf16[16640,2048]{1,0:T(8,128)(2,1)} async-done(((bf16[1040,2048]{1,0:T(8,128)(2,1)}), bf16[16640,2048]{1,0:T(8,128)(2,1)}) %all-gather.5.cloned.1.call-update) | async-done | bytes 68157456 | tf_op jit(solution)/shard_map/all_gather | solution.py:189
  961.1 24.6 %reduce_sum.104 = bf16[1040,2048]{1,0:T(8,128)(2,1)} reduce(bf16[16,1040,2048]{2,1,0:T(8,128)(2,1)} %bitcast.45, bf16[]{:T(256)} %constant.131.clone.1), dimensions={0}, to_apply=%region_17.18 | reduce | flops 31948800 | bytes 72417280 | tf_op jit(solution)/shard_map/reduce_sum | solution.py:189
  (323 shorter events, 169.5 us)
Async XLA Ops:
  7.2 48.0 %copy-start = (bf16[48,128,128]{2,1,0:T(8,128)(2,1)S(1)}, bf16[48,128,128]{2,1,0:T(8,128)(2,1)}, u32[]{:S(2)}) copy-start(bf16[48,128,128]{2,1,0:T(8,128)(2,1)} %param.28) | copy-start | bytes 4718596
  8.1 12.7 %copy-start.11 = (s32[16]{0:T(128)}, s32[16]{0:T(128)S(1)}, u32[]{:S(2)}) copy-start(s32[16]{0:T(128)S(1)} %select_reduce_fusion) | copy-start | bytes 196
  32.4 17.1 %copy-start.9 = (s32[16]{0:T(128)S(1)}, s32[16]{0:T(128)}, u32[]{:S(2)}) copy-start(s32[16]{0:T(128)} %param.31) | copy-start | bytes 196
  32.4 18.2 %copy-start.10 = (s32[128]{0:T(128)S(1)}, s32[128]{0:T(128)}, u32[]{:S(2)}) copy-start(s32[128]{0:T(128)} %param.35) | copy-start | bytes 1540
  32.5 20.4 %copy-start.8 = (u32[128]{0:T(128)S(1)}, u32[128]{0:T(128)}, u32[]{:S(2)}) copy-start(u32[128]{0:T(128)} %constant.189) | copy-start | bytes 1540
  36.3 25.3 %all-to-all-start = ((bf16[16,2,15360]{2,1,0:T(2,128)(2,1)}), bf16[16,2,15360]{2,1,0:T(2,128)(2,1)}, u32[]{:S(2)}, u32[]{:S(2)}) async-start(bf16[16,2,15360]{2,1,0:T(2,128)(2,1)} %reshape.374), calls=%async_computation | async-start | bytes 1966080 | tf_op jit(solution)/shard_map/all_to_all | solution.py:73
  61.6 5.9 copy-start.13
  387.3 3.3 copy-start.2
  397.3 4.3 copy-start.3
  397.3 4.3 copy-start.4
  406.4 3.3 copy-start.2
  416.4 4.3 copy-start.3
  416.4 4.3 copy-start.4
  425.4 3.3 copy-start.2
  435.4 4.3 copy-start.3
  435.4 4.3 copy-start.4
  444.4 3.3 copy-start.2
  454.4 4.3 copy-start.3
  454.4 4.3 copy-start.4
  460.3 20.2 %copy-start.6 = (pred[8]{0:T(512)(128)(4,1)S(1)}, pred[8]{0:T(512)(128)(4,1)}, u32[]{:S(2)}) copy-start(pred[8]{0:T(512)(128)(4,1)} %get-tuple-element.149) | copy-start | bytes 28
  462.8 19.2 %copy-start.7 = (pred[4,4]{1,0:T(4,128)(4,1)S(1)}, pred[4,4]{1,0:T(4,128)(4,1)}, u32[]{:S(2)}) copy-start(pred[4,4]{1,0:T(4,128)(4,1)} %broadcast_in_dim.177) | copy-start | bytes 52
  464.6 14.6 %all-to-all-start.1 = ((bf16[16,2,5120]{2,1,0:T(2,128)(2,1)}), bf16[16,2,5120]{2,1,0:T(2,128)(2,1)S(1)}, u32[]{:S(2)}, u32[]{:S(2)}) async-start(bf16[16,2,5120]{2,1,0:T(2,128)(2,1)} %reshape.376), calls=%async_computation.1 | async-start | bytes 655360 | tf_op jit(solution)/shard_map/all_to_all | solution.py:157
  471.3 95.8 %all-gather.7.cloned.1.call-start = ((), (), s32[]{:S(2)}) async-start(), calls=%async_computation.3 | async-start | bytes 5013504 | tf_op jit(solution)/shard_map/all_gather | solution.py:185
  483.0 30.9 %copy-start.5 = (f32[2048]{0:T(1024)S(1)}, f32[2048]{0:T(1024)}, u32[]{:S(2)}) copy-start(f32[2048]{0:T(1024)} %param.25) | copy-start | bytes 24580
  506.3 6.8 collective-permute-start
  514.8 446.3 %all-gather.5.cloned.1.call-start = ((), (), s32[]{:S(2)}) async-start(), calls=%async_computation.2 | async-start | bytes 72417280 | tf_op jit(solution)/shard_map/all_gather | solution.py:189
  571.6 5.7 copy-start.12
  961.1 27.1 %copy-start.1 = (bf16[48,128,128]{2,1,0:T(8,128)(2,1)S(1)}, bf16[48,128,128]{2,1,0:T(8,128)(2,1)}, u32[]{:S(2)}) copy-start(bf16[48,128,128]{2,1,0:T(8,128)(2,1)} %param.28) | copy-start | bytes 4718596
Sparse Core Ops, SparseCore 0:
  514.9 52.1 all-gather.6
  587.4 373.5 all-gather.4
